TPU v7x, 128 devices: a whole 4x4x4 slice. The times are simulated.
128 devices in a mesh: tiles: 64 (over y, z_hi, x, core), vec: 2 (over z_lo).
Axes of the slice: x: 4, y: 4, z: 4 (z_hi: 2, z_lo: 2; z = z_hi * 2 + z_lo), core: 2. Of those that a mesh axis runs over, the one named last changes fastest.
Arguments:
- omega: float32 [128, 4, 512, 128], P('vec', None, 'tiles'), may hold values from -24 to 24
- conductance: float32 [3, 4, 512, 128], P(None, None, 'tiles'), may hold values from 0.02 to 0.16
- wet: int32 [512, 128], P('tiles'), may hold values 0 or 1
- volume: float32 [512, 128], P('tiles'), may hold values from 0.3 to 27, as said below
- face_runs: int32 [64, 4], P('tiles'), may hold values from 0 to 128, as said below
Outputs:
- diffused: float32 [128, 4, 512, 128], P('vec', None, 'tiles')
- r_factor: float32 [128, 128], replicated
Inputs may be any that keep to these rules, and one draw needn't show every extreme that they name: `face_runs`: tiles in tile row 0 have a closed lower row face and tiles in tile column 0 a closed lower column face (length 0); every other run lies within its face, covers at least half of it, and some tiles have fully open faces. Positive cell volume weights.
All inputs are finite; a program needn't handle non-finite values. No bound on the sum of `wet` on one device may be relied on, other than what follows from the above.
Results may differ from a plain program's by a relative error of at most 0.00005.
Values sent between devices are 32-bit elements; how exact they have to be, the bound alone decides.
A program may use at most 64 MiB of HBM per device.

v0:
```python
import jax
import jax.numpy as jnp
from jax import lax
from jax.sharding import PartitionSpec as P

TGY = 8
ITERS = 4


def shifted(value, axis, steps):
    count = lax.axis_size(axis)
    first, last = (max(0, -steps), min(count, count - steps))
    return lax.ppermute(value, axis, [(source, source + steps) for source in range(first, last)])


def diffuse(field, statics):
    cond_x = statics[0]
    cond_y = statics[1]
    cond_z = statics[2]
    wet_cells = statics[3]
    flux_x = cond_x[:, 1:, :] * (field[:, :, 1:, :] - field[:, :, :-1, :])
    flux_y = cond_y[:, :, 1:] * (field[:, :, :, 1:] - field[:, :, :, :-1])
    flux_z = cond_z[1:] * (field[:, 1:] - field[:, :-1])
    zero_level = jnp.zeros_like(field[:, :1])
    flux_z = jnp.concatenate([zero_level, flux_z, zero_level], axis=1)
    change = flux_x[:, :, 1:, 1:-1] - flux_x[:, :, :-1, 1:-1]
    change = change + flux_y[:, :, 1:-1, 1:] - flux_y[:, :, 1:-1, :-1]
    change = change + (flux_z[:, 1:] - flux_z[:, :-1])[:, :, 1:-1, 1:-1]
    return wet_cells[:, 1:-1, 1:-1] * (field[:, :, 1:-1, 1:-1] + change)


def moving(values, offset):
    return shifted(values, "tiles", offset)


def fixed_rim(values, offset):
    return shifted(values, "tiles", offset)


def extend(values, margin, neighbour):
    lower_rim = neighbour(values[:, :, -margin:, :], TGY)
    upper_rim = neighbour(values[:, :, :margin, :], -TGY)
    stacked = jnp.concatenate([lower_rim, values, upper_rim], axis=2)
    left_rim = neighbour(stacked[:, :, :, -margin:], 1)
    right_rim = neighbour(stacked[:, :, :, :margin], -1)
    return jnp.concatenate([left_rim, stacked, right_rim], axis=3)


def shards(omega, conductance, wet, volume, face_runs):
    levels = omega.shape[1]
    tile_rows = omega.shape[2]
    tile_cols = omega.shape[3]
    row_ids = lax.broadcasted_iota(jnp.int32, (tile_rows, tile_cols), 0)
    col_ids = lax.broadcasted_iota(jnp.int32, (tile_rows, tile_cols), 1)
    runs = face_runs[0]
    open_x = (col_ids >= runs[0]) & (col_ids < runs[0] + runs[1])
    factor_x = jnp.where(row_ids == 0, open_x.astype(jnp.float32), jnp.float32(1.0))
    open_y = (row_ids >= runs[2]) & (row_ids < runs[2] + runs[3])
    factor_y = jnp.where(col_ids == 0, open_y.astype(jnp.float32), jnp.float32(1.0))
    level_ids = lax.broadcasted_iota(jnp.int32, (levels, 1, 1), 0)
    cond_z = conductance[2] * (level_ids > 0).astype(jnp.float32)
    wet_float = wet.astype(jnp.float32)
    statics = jnp.stack(
        [
            conductance[0] * factor_x[None],
            conductance[1] * factor_y[None],
            cond_z,
            jnp.broadcast_to(wet_float[None], (levels, tile_rows, tile_cols)),
        ]
    )
    margin = 1
    statics_wide = extend(statics, margin, fixed_rim)
    field = wet_float[None, None] * omega
    for block_index in range(ITERS // margin):
        grown = extend(field, margin, moving)
        current = statics_wide
        grown = diffuse(grown, current)
        current = current[:, :, 1:-1, 1:-1]
        field = grown
    regrouped = lax.all_to_all(field, "vec", split_axis=1, concat_axis=0, tiled=True)
    all_vectors = regrouped.shape[0]
    total_cells = levels * lax.axis_size("tiles") * tile_rows * tile_cols
    flat_values = regrouped.reshape(all_vectors, -1)
    weighted = (regrouped * volume[None, None]).reshape(all_vectors, -1)
    gram_local = (
        lax.dot_general(
            weighted,
            flat_values,
            (((1,), (1,)), ((), ())),
            precision=lax.Precision.HIGHEST,
            preferred_element_type=jnp.float32,
        )
        / total_cells
    )
    gram = lax.psum(gram_local, ("tiles", "vec"))
    r_factor = jnp.linalg.cholesky(gram).T
    return (field, r_factor)


def solution(mesh):
    in_specs = (
        P("vec", None, "tiles", None),
        P(None, None, "tiles", None),
        P("tiles", None),
        P("tiles", None),
        P("tiles", None),
    )
    out_specs = (P("vec", None, "tiles", None), P())
    return jax.shard_map(shards, mesh=mesh, in_specs=in_specs, out_specs=out_specs, check_vma=False)
```

profile of v0, /device:TPU:1, one launch (start us, length us, event | category | flops | bytes accessed | tf_op | source)
XLA Modules:
  0.0 363.9 jit_solution(15413979670254158427)
XLA Ops:
  7.2 1.5 fusion.34
  13.2 0.8 slice_multiply_fusion.2
  14.1 6.3 %collective-permute-start = (f32[4,4,1,128]{3,2,1,0:T(1,128)S(1)}, f32[4,4,1,128]{3,2,1,0:T(1,128)S(1)}, u32[]{:S(2)}, u32[]{:S(2)}) collective-permute-start(f32[4,4,1,128]{3,2,1,0:T(1,128)S(1)} %get-tuple-element.29), channel_id=1, source_target_pairs={{0,16},{2,18},{4,20},{6,22},{8,24},{10,26},{12,28},{14,30},{16,32}... | collective-permute-start | bytes 24584 | tf_op jit(solution)/shard_map/ppermute | solution.py:13
  20.4 1.3 collective-permute-start.1
  21.7 1.8 copy_multiply_fusion
  23.6 2.7 collective-permute-done.1
  26.4 5.1 %collective-permute-start.2 = (f32[4,4,10,1]{3,2,1,0:T(8,128)S(1)}, f32[4,4,10,1]{3,2,1,0:T(8,128)S(1)}, u32[]{:S(2)}, u32[]{:S(2)}) collective-permute-start(f32[4,4,10,1]{3,2,1,0:T(8,128)S(1)} %get-tuple-element.27), channel_id=1, source_target_pairs={{0,2},{2,4},{4,6},{6,8},{8,10},{10,12},{12,14},{14,16},{16,18},{18... | collective-permute-start | bytes 1928 | tf_op jit(solution)/shard_map/ppermute | solution.py:13
  31.6 1.9 collective-permute-start.3
  33.5 3.2 collective-permute-start.4
  36.7 1.3 collective-permute-start.5
  38.6 5.3 %collective-permute-done.5 = f32[64,4,1,128]{3,0,2,1:T(8,128)S(1)} collective-permute-done((f32[64,4,1,128]{3,0,2,1:T(8,128)S(1)}, f32[64,4,1,128]{3,0,2,1:T(8,128)S(1)}, u32[]{:S(2)}, u32[]{:S(2)}) %collective-permute-start.5) | collective-permute-done | bytes 131104 | tf_op jit(solution)/shard_map/ppermute | solution.py:13
  44.0 1.5 fusion.28
  45.6 2.0 copy.15
  48.3 8.0 %collective-permute-start.7 = (f32[64,4,10,1]{0,2,3,1:T(8,128)S(1)}, f32[64,4,10,1]{0,2,3,1:T(8,128)S(1)}, u32[]{:S(2)}, u32[]{:S(2)}) collective-permute-start(f32[64,4,10,1]{0,2,3,1:T(8,128)S(1)} %copy.16), channel_id=1, source_target_pairs={{2,0},{4,2},{6,4},{8,6},{10,8},{12,10},{14,12},{16,14},{18,16},{20... | collective-permute-start | bytes 30728 | tf_op jit(solution)/shard_map/ppermute | solution.py:13
  56.2 1.9 collective-permute-start.6
  58.4 1.0 collective-permute-done.6
  59.8 1.6 copy.18
  61.4 2.4 pad_maximum_fusion
  64.6 0.9 copy-done.1
  65.5 0.8 fusion
  66.7 1.3 fusion.23
  68.0 6.0 %collective-permute-start.8 = (f32[64,4,1,128]{3,0,2,1:T(8,128)S(1)}, f32[64,4,1,128]{3,0,2,1:T(8,128)S(1)}, u32[]{:S(2)}, u32[]{:S(2)}) collective-permute-start(f32[64,4,1,128]{3,0,2,1:T(8,128)S(1)} %get-tuple-element.20), channel_id=1, source_target_pairs={{0,16},{2,18},{4,20},{6,22},{8,24},{10,26},{12,28},{14,30},{16,32}... | collective-permute-start | bytes 393224 | tf_op jit(solution)/shard_map/ppermute | solution.py:13
  74.1 1.3 collective-permute-start.9
  76.0 5.3 %collective-permute-done.9 = f32[64,4,1,128]{3,0,2,1:T(8,128)S(1)} collective-permute-done((f32[64,4,1,128]{3,0,2,1:T(8,128)S(1)}, f32[64,4,1,128]{3,0,2,1:T(8,128)S(1)}, u32[]{:S(2)}, u32[]{:S(2)}) %collective-permute-start.9) | collective-permute-done | bytes 131104 | tf_op jit(solution)/shard_map/ppermute | solution.py:13
  81.4 1.5 fusion.27
  82.9 2.0 copy.21
  84.9 5.5 %collective-permute-start.10 = (f32[64,4,10,1]{0,2,3,1:T(8,128)S(1)}, f32[64,4,10,1]{0,2,3,1:T(8,128)S(1)}, u32[]{:S(2)}, u32[]{:S(2)}) collective-permute-start(f32[64,4,10,1]{0,2,3,1:T(8,128)S(1)} %copy.21), channel_id=1, source_target_pairs={{0,2},{2,4},{4,6},{6,8},{8,10},{10,12},{12,14},{14,16},{16,18},{18... | collective-permute-start | bytes 30728 | tf_op jit(solution)/shard_map/ppermute | solution.py:13
  91.1 5.1 %collective-permute-start.11 = (f32[64,4,10,1]{0,2,3,1:T(8,128)S(1)}, f32[64,4,10,1]{0,2,3,1:T(8,128)S(1)}, u32[]{:S(2)}, u32[]{:S(2)}) collective-permute-start(f32[64,4,10,1]{0,2,3,1:T(8,128)S(1)} %copy.22), channel_id=1, source_target_pairs={{2,0},{4,2},{6,4},{8,6},{10,8},{12,10},{14,12},{16,14},{18,16},{20... | collective-permute-start | bytes 30728 | tf_op jit(solution)/shard_map/ppermute | solution.py:13
  96.9 1.6 copy.24
  98.4 2.4 pad_maximum_fusion.1
  101.6 0.9 copy-done.2
  103.3 1.3 fusion.20
  104.7 4.5 %collective-permute-start.12 = (f32[64,4,1,128]{3,0,2,1:T(8,128)S(1)}, f32[64,4,1,128]{3,0,2,1:T(8,128)S(1)}, u32[]{:S(2)}, u32[]{:S(2)}) collective-permute-start(f32[64,4,1,128]{3,0,2,1:T(8,128)S(1)} %get-tuple-element.18), channel_id=1, source_target_pairs={{0,16},{2,18},{4,20},{6,22},{8,24},{10,26},{12,28},{14,30},{16,32}... | collective-permute-start | bytes 393224 | tf_op jit(solution)/shard_map/ppermute | solution.py:13
  109.2 1.3 collective-permute-start.13
  111.1 5.3 %collective-permute-done.13 = f32[64,4,1,128]{3,0,2,1:T(8,128)S(1)} collective-permute-done((f32[64,4,1,128]{3,0,2,1:T(8,128)S(1)}, f32[64,4,1,128]{3,0,2,1:T(8,128)S(1)}, u32[]{:S(2)}, u32[]{:S(2)}) %collective-permute-start.13) | collective-permute-done | bytes 131104 | tf_op jit(solution)/shard_map/ppermute | solution.py:13
  116.5 1.5 fusion.26
  118.0 2.0 copy.27
  120.0 1.9 collective-permute-start.14
  122.6 8.8 %collective-permute-start.15 = (f32[64,4,10,1]{0,2,3,1:T(8,128)S(1)}, f32[64,4,10,1]{0,2,3,1:T(8,128)S(1)}, u32[]{:S(2)}, u32[]{:S(2)}) collective-permute-start(f32[64,4,10,1]{0,2,3,1:T(8,128)S(1)} %copy.28), channel_id=1, source_target_pairs={{2,0},{4,2},{6,4},{8,6},{10,8},{12,10},{14,12},{16,14},{18,16},{20... | collective-permute-start | bytes 30728 | tf_op jit(solution)/shard_map/ppermute | solution.py:13
  132.3 1.6 copy.30
  133.8 2.4 pad_maximum_fusion.2
  137.1 0.9 copy-done.3
  138.8 1.3 fusion.17
  140.1 6.4 %collective-permute-start.16 = (f32[64,4,1,128]{3,0,2,1:T(8,128)S(1)}, f32[64,4,1,128]{3,0,2,1:T(8,128)S(1)}, u32[]{:S(2)}, u32[]{:S(2)}) collective-permute-start(f32[64,4,1,128]{3,0,2,1:T(8,128)S(1)} %get-tuple-element.16), channel_id=1, source_target_pairs={{0,16},{2,18},{4,20},{6,22},{8,24},{10,26},{12,28},{14,30},{16,32}... | collective-permute-start | bytes 393224 | tf_op jit(solution)/shard_map/ppermute | solution.py:13
  146.5 1.3 collective-permute-start.17
  148.4 5.3 %collective-permute-done.17 = f32[64,4,1,128]{3,0,2,1:T(8,128)S(1)} collective-permute-done((f32[64,4,1,128]{3,0,2,1:T(8,128)S(1)}, f32[64,4,1,128]{3,0,2,1:T(8,128)S(1)}, u32[]{:S(2)}, u32[]{:S(2)}) %collective-permute-start.17) | collective-permute-done | bytes 131104 | tf_op jit(solution)/shard_map/ppermute | solution.py:13
  153.8 1.5 fusion.25
  155.3 2.0 copy.33
  157.3 1.9 collective-permute-start.18
  159.9 9.0 %collective-permute-start.19 = (f32[64,4,10,1]{0,2,3,1:T(8,128)S(1)}, f32[64,4,10,1]{0,2,3,1:T(8,128)S(1)}, u32[]{:S(2)}, u32[]{:S(2)}) collective-permute-start(f32[64,4,10,1]{0,2,3,1:T(8,128)S(1)} %copy.34), channel_id=1, source_target_pairs={{2,0},{4,2},{6,4},{8,6},{10,8},{12,10},{14,12},{16,14},{18,16},{20... | collective-permute-start | bytes 30728 | tf_op jit(solution)/shard_map/ppermute | solution.py:13
  169.6 1.6 copy.36
  171.1 2.4 pad_maximum_fusion.3
  174.3 0.9 copy-done
  176.0 1.3 fusion.14
  178.0 15.8 %all_to_all.15 = f32[64,4,8,128]{3,2,0,1:T(8,128)S(1)} all-to-all(f32[64,4,8,128]{3,2,0,1:T(8,128)S(1)} %copy.39), channel_id=1, replica_groups=mesh['tiles'=64,'vec'=2] {'vec'}, dimensions={1} | all-to-all | bytes 2097152 | tf_op jit(solution)/shard_map/all_to_all | solution.py:80
  193.8 1.1 copy.52
  194.9 1.4 reshape.96
  196.3 1.1 mul.184
  197.5 2.9 convolution_multiply_fusion
  200.3 1.6 copy.43
  201.9 139.6 %all-reduce.10.cloned.1.call-done = f32[128,128]{0,1:T(8,128)} async-done(((f32[128,128]{0,1:T(8,128)}), f32[128,128]{0,1:T(8,128)}) %all-reduce.10.cloned.1.call-update) | async-done | bytes 65552 | tf_op jit(solution)/shard_map/psum | solution.py:95
  341.5 0.9 copy.42
  342.4 0.9 fusion.24
  343.3 11.7 %cholesky.18 = f32[128,128]{1,0:T(8,128)S(1)} custom-call(f32[128,128]{1,0:T(8,128)S(1)} %fusion.24), custom_call_target="Cholesky" | custom-call | tf_op jit(solution)/shard_map/jit(cholesky)/cholesky | solution.py:96
  (80 shorter events, 19.2 us)
Async XLA Ops:
  7.2 334.3 %all-reduce.10.cloned.1.call-start = ((), (), s32[]{:S(2)}) async-start(), calls=%async_computation.1 | async-start | bytes 131072 | tf_op jit(solution)/shard_map/psum | solution.py:95
  14.1 9.5 %collective-permute-start = (f32[4,4,1,128]{3,2,1,0:T(1,128)S(1)}, f32[4,4,1,128]{3,2,1,0:T(1,128)S(1)}, u32[]{:S(2)}, u32[]{:S(2)}) collective-permute-start(f32[4,4,1,128]{3,2,1,0:T(1,128)S(1)} %get-tuple-element.29), channel_id=1, source_target_pairs={{0,16},{2,18},{4,20},{6,22},{8,24},{10,26},{12,28},{14,30},{16,32}... | collective-permute-start | bytes 24584 | tf_op jit(solution)/shard_map/ppermute | solution.py:13
  20.4 5.9 %collective-permute-start.1 = (f32[4,4,1,128]{3,2,1,0:T(1,128)S(1)}, f32[4,4,1,128]{3,2,1,0:T(1,128)S(1)}, u32[]{:S(2)}, u32[]{:S(2)}) collective-permute-start(f32[4,4,1,128]{3,2,1,0:T(1,128)S(1)} %get-tuple-element.30), channel_id=1, source_target_pairs={{16,0},{18,2},{20,4},{22,6},{24,8},{26,10},{28,12},{30,14},{32,16}... | collective-permute-start | bytes 24584 | tf_op jit(solution)/shard_map/ppermute | solution.py:13
  26.4 11.6 %collective-permute-start.2 = (f32[4,4,10,1]{3,2,1,0:T(8,128)S(1)}, f32[4,4,10,1]{3,2,1,0:T(8,128)S(1)}, u32[]{:S(2)}, u32[]{:S(2)}) collective-permute-start(f32[4,4,10,1]{3,2,1,0:T(8,128)S(1)} %get-tuple-element.27), channel_id=1, source_target_pairs={{0,2},{2,4},{4,6},{6,8},{8,10},{10,12},{12,14},{14,16},{16,18},{18... | collective-permute-start | bytes 1928 | tf_op jit(solution)/shard_map/ppermute | solution.py:13
  31.6 6.5 %collective-permute-start.3 = (f32[4,4,10,1]{3,2,1,0:T(8,128)S(1)}, f32[4,4,10,1]{3,2,1,0:T(8,128)S(1)}, u32[]{:S(2)}, u32[]{:S(2)}) collective-permute-start(f32[4,4,10,1]{3,2,1,0:T(8,128)S(1)} %get-tuple-element.28), channel_id=1, source_target_pairs={{2,0},{4,2},{6,4},{8,6},{10,8},{12,10},{14,12},{16,14},{18,16},{20... | collective-permute-start | bytes 1928 | tf_op jit(solution)/shard_map/ppermute | solution.py:13
  33.5 5.1 %collective-permute-start.4 = (f32[64,4,1,128]{3,0,2,1:T(8,128)S(1)}, f32[64,4,1,128]{3,0,2,1:T(8,128)S(1)}, u32[]{:S(2)}, u32[]{:S(2)}) collective-permute-start(f32[64,4,1,128]{3,0,2,1:T(8,128)S(1)} %get-tuple-element.22), channel_id=1, source_target_pairs={{0,16},{2,18},{4,20},{6,22},{8,24},{10,26},{12,28},{14,30},{16,32}... | collective-permute-start | bytes 393224 | tf_op jit(solution)/shard_map/ppermute | solution.py:13
  36.7 7.2 %collective-permute-start.5 = (f32[64,4,1,128]{3,0,2,1:T(8,128)S(1)}, f32[64,4,1,128]{3,0,2,1:T(8,128)S(1)}, u32[]{:S(2)}, u32[]{:S(2)}) collective-permute-start(f32[64,4,1,128]{3,0,2,1:T(8,128)S(1)} %get-tuple-element.23), channel_id=1, source_target_pairs={{16,0},{18,2},{20,4},{22,6},{24,8},{26,10},{28,12},{30,14},{32,16}... | collective-permute-start | bytes 393224 | tf_op jit(solution)/shard_map/ppermute | solution.py:13
  48.3 11.5 %collective-permute-start.7 = (f32[64,4,10,1]{0,2,3,1:T(8,128)S(1)}, f32[64,4,10,1]{0,2,3,1:T(8,128)S(1)}, u32[]{:S(2)}, u32[]{:S(2)}) collective-permute-start(f32[64,4,10,1]{0,2,3,1:T(8,128)S(1)} %copy.16), channel_id=1, source_target_pairs={{2,0},{4,2},{6,4},{8,6},{10,8},{12,10},{14,12},{16,14},{18,16},{20... | collective-permute-start | bytes 30728 | tf_op jit(solution)/shard_map/ppermute | solution.py:13
  56.2 3.1 collective-permute-start.6
  58.2 42.7 %copy-start.5 = (f32[3,10,130]{2,1,0:T(8,128)}, f32[3,10,130]{2,1,0:T(8,128)S(1)}, u32[]{:S(2)}) copy-start(f32[3,10,130]{2,1,0:T(8,128)S(1)} %slice_bitcast_fusion.3) | copy-start | bytes 46804
  64.1 1.3 copy-start.1
  65.5 1.2 copy-start.4
  68.0 8.0 %collective-permute-start.8 = (f32[64,4,1,128]{3,0,2,1:T(8,128)S(1)}, f32[64,4,1,128]{3,0,2,1:T(8,128)S(1)}, u32[]{:S(2)}, u32[]{:S(2)}) collective-permute-start(f32[64,4,1,128]{3,0,2,1:T(8,128)S(1)} %get-tuple-element.20), channel_id=1, source_target_pairs={{0,16},{2,18},{4,20},{6,22},{8,24},{10,26},{12,28},{14,30},{16,32}... | collective-permute-start | bytes 393224 | tf_op jit(solution)/shard_map/ppermute | solution.py:13
  74.1 7.2 %collective-permute-start.9 = (f32[64,4,1,128]{3,0,2,1:T(8,128)S(1)}, f32[64,4,1,128]{3,0,2,1:T(8,128)S(1)}, u32[]{:S(2)}, u32[]{:S(2)}) collective-permute-start(f32[64,4,1,128]{3,0,2,1:T(8,128)S(1)} %get-tuple-element.21), channel_id=1, source_target_pairs={{16,0},{18,2},{20,4},{22,6},{24,8},{26,10},{28,12},{30,14},{32,16}... | collective-permute-start | bytes 393224 | tf_op jit(solution)/shard_map/ppermute | solution.py:13
  84.9 11.3 %collective-permute-start.10 = (f32[64,4,10,1]{0,2,3,1:T(8,128)S(1)}, f32[64,4,10,1]{0,2,3,1:T(8,128)S(1)}, u32[]{:S(2)}, u32[]{:S(2)}) collective-permute-start(f32[64,4,10,1]{0,2,3,1:T(8,128)S(1)} %copy.21), channel_id=1, source_target_pairs={{0,2},{2,4},{4,6},{6,8},{8,10},{10,12},{12,14},{14,16},{16,18},{18... | collective-permute-start | bytes 30728 | tf_op jit(solution)/shard_map/ppermute | solution.py:13
  91.1 5.8 %collective-permute-start.11 = (f32[64,4,10,1]{0,2,3,1:T(8,128)S(1)}, f32[64,4,10,1]{0,2,3,1:T(8,128)S(1)}, u32[]{:S(2)}, u32[]{:S(2)}) collective-permute-start(f32[64,4,10,1]{0,2,3,1:T(8,128)S(1)} %copy.22), channel_id=1, source_target_pairs={{2,0},{4,2},{6,4},{8,6},{10,8},{12,10},{14,12},{16,14},{18,16},{20... | collective-permute-start | bytes 30728 | tf_op jit(solution)/shard_map/ppermute | solution.py:13
  101.2 1.3 copy-start.2
  104.7 6.4 %collective-permute-start.12 = (f32[64,4,1,128]{3,0,2,1:T(8,128)S(1)}, f32[64,4,1,128]{3,0,2,1:T(8,128)S(1)}, u32[]{:S(2)}, u32[]{:S(2)}) collective-permute-start(f32[64,4,1,128]{3,0,2,1:T(8,128)S(1)} %get-tuple-element.18), channel_id=1, source_target_pairs={{0,16},{2,18},{4,20},{6,22},{8,24},{10,26},{12,28},{14,30},{16,32}... | collective-permute-start | bytes 393224 | tf_op jit(solution)/shard_map/ppermute | solution.py:13
  109.2 7.2 %collective-permute-start.13 = (f32[64,4,1,128]{3,0,2,1:T(8,128)S(1)}, f32[64,4,1,128]{3,0,2,1:T(8,128)S(1)}, u32[]{:S(2)}, u32[]{:S(2)}) collective-permute-start(f32[64,4,1,128]{3,0,2,1:T(8,128)S(1)} %get-tuple-element.19), channel_id=1, source_target_pairs={{16,0},{18,2},{20,4},{22,6},{24,8},{26,10},{28,12},{30,14},{32,16}... | collective-permute-start | bytes 393224 | tf_op jit(solution)/shard_map/ppermute | solution.py:13
  120.0 11.4 %collective-permute-start.14 = (f32[64,4,10,1]{0,2,3,1:T(8,128)S(1)}, f32[64,4,10,1]{0,2,3,1:T(8,128)S(1)}, u32[]{:S(2)}, u32[]{:S(2)}) collective-permute-start(f32[64,4,10,1]{0,2,3,1:T(8,128)S(1)} %copy.27), channel_id=1, source_target_pairs={{0,2},{2,4},{4,6},{6,8},{8,10},{10,12},{12,14},{14,16},{16,18},{18... | collective-permute-start | bytes 30728 | tf_op jit(solution)/shard_map/ppermute | solution.py:13
  122.6 9.6 %collective-permute-start.15 = (f32[64,4,10,1]{0,2,3,1:T(8,128)S(1)}, f32[64,4,10,1]{0,2,3,1:T(8,128)S(1)}, u32[]{:S(2)}, u32[]{:S(2)}) collective-permute-start(f32[64,4,10,1]{0,2,3,1:T(8,128)S(1)} %copy.28), channel_id=1, source_target_pairs={{2,0},{4,2},{6,4},{8,6},{10,8},{12,10},{14,12},{16,14},{18,16},{20... | collective-permute-start | bytes 30728 | tf_op jit(solution)/shard_map/ppermute | solution.py:13
  133.8 2.4 copy-start.6
  136.6 1.3 copy-start.3
  140.1 8.3 %collective-permute-start.16 = (f32[64,4,1,128]{3,0,2,1:T(8,128)S(1)}, f32[64,4,1,128]{3,0,2,1:T(8,128)S(1)}, u32[]{:S(2)}, u32[]{:S(2)}) collective-permute-start(f32[64,4,1,128]{3,0,2,1:T(8,128)S(1)} %get-tuple-element.16), channel_id=1, source_target_pairs={{0,16},{2,18},{4,20},{6,22},{8,24},{10,26},{12,28},{14,30},{16,32}... | collective-permute-start | bytes 393224 | tf_op jit(solution)/shard_map/ppermute | solution.py:13
  146.5 7.2 %collective-permute-start.17 = (f32[64,4,1,128]{3,0,2,1:T(8,128)S(1)}, f32[64,4,1,128]{3,0,2,1:T(8,128)S(1)}, u32[]{:S(2)}, u32[]{:S(2)}) collective-permute-start(f32[64,4,1,128]{3,0,2,1:T(8,128)S(1)} %get-tuple-element.17), channel_id=1, source_target_pairs={{16,0},{18,2},{20,4},{22,6},{24,8},{26,10},{28,12},{30,14},{32,16}... | collective-permute-start | bytes 393224 | tf_op jit(solution)/shard_map/ppermute | solution.py:13
  157.3 11.7 %collective-permute-start.18 = (f32[64,4,10,1]{0,2,3,1:T(8,128)S(1)}, f32[64,4,10,1]{0,2,3,1:T(8,128)S(1)}, u32[]{:S(2)}, u32[]{:S(2)}) collective-permute-start(f32[64,4,10,1]{0,2,3,1:T(8,128)S(1)} %copy.33), channel_id=1, source_target_pairs={{0,2},{2,4},{4,6},{6,8},{8,10},{10,12},{12,14},{14,16},{16,18},{18... | collective-permute-start | bytes 30728 | tf_op jit(solution)/shard_map/ppermute | solution.py:13
  159.9 9.6 %collective-permute-start.19 = (f32[64,4,10,1]{0,2,3,1:T(8,128)S(1)}, f32[64,4,10,1]{0,2,3,1:T(8,128)S(1)}, u32[]{:S(2)}, u32[]{:S(2)}) collective-permute-start(f32[64,4,10,1]{0,2,3,1:T(8,128)S(1)} %copy.34), channel_id=1, source_target_pairs={{2,0},{4,2},{6,4},{8,6},{10,8},{12,10},{14,12},{16,14},{18,16},{20... | collective-permute-start | bytes 30728 | tf_op jit(solution)/shard_map/ppermute | solution.py:13
  171.1 2.4 copy-start.7
  173.9 1.3 copy-start
  178.0 16.9 %copy-start.8 = (f32[8,128]{1,0:T(8,128)S(1)}, f32[8,128]{1,0:T(8,128)}, u32[]{:S(2)}) copy-start(f32[8,128]{1,0:T(8,128)} %param.8) | copy-start | bytes 12292
Sparse Core Ops, SparseCore 0:
  200.5 140.9 all-reduce.9
where the time goes:
time: 365 us; the launch traced here: 364 us
  waiting for transfers between devices  167 us (46%)
  starting transfers between devices  82.1 us (22%)
  other arithmetic  40.4 us (11%)
  local copies, waits for them, and re-layouts  38.2 us (10%)
  between operations  17.2 us (5%)
  blocking collectives  15.8 us (4%)
    psum x1, waiting for transfers between devices, shards(): gram = lax.psum(gram_local, ('tiles', 'vec'))  140 us
    ppermute x20, starting transfers between devices, shifted(): lax.ppermute(value, axis, [(source, source + steps) for source in range(f...  82 us
    ppermute x20, waiting for transfers between devices, shifted(): lax.ppermute(value, axis, [(source, source + steps) for source in range(f...  27.8 us
    all_to_all x1, blocking collectives, shards(): lax.all_to_all(field, 'vec', split_axis=1, concat_axis=0, tiled=True)  15.8 us
    slice x9, local copies, waits for them, and re-layouts, extend(): left_rim = neighbour(stacked[:, :, :, -margin:], 1)  14.2 us
    another operation x3, other arithmetic, shards(): r_factor = jnp.linalg.cholesky(gram).T  12.4 us
    concatenate x5, other arithmetic, extend(): return jnp.concatenate([left_rim, stacked, right_rim], axis=3)  9.82 us
    ppermute x8, local copies, waits for them, and re-layouts, shifted(): lax.ppermute(value, axis, [(source, source + steps) for source in range(f...  8.08 us
  transfers between devices with their start and end apart: 21, of which 14 were waited for; matrix products, arithmetic and copies ran while one was open for 2% of the time, Pallas kernels for 0%

commit v1 on v0

--- a/solution.py
+++ b/solution.py
@@ -92,7 +92,7 @@
         )
         / total_cells
     )
-    gram = lax.psum(gram_local, ("tiles", "vec"))
+    gram = lax.psum(lax.psum(gram_local, "tiles"), "vec")
     r_factor = jnp.linalg.cholesky(gram).T
     return (field, r_factor)
 

time: 365 us -> 817 us (2.24)
  waiting for transfers between devices: 167 us -> 619 us
    psum x1 -> x2, waiting for transfers between devices: 140 us -> 592 us  [shards(): gram = lax.psum(lax.psum(gram_local, 'tiles'), 'vec')]
  transfers between devices with their start and end apart: 21 -> 22, of which waited for: 14 -> 15; matrix products, arithmetic and copies ran while one was open for 2% -> 1% of each run, Pallas kernels for 0% -> 0%
where the time goes in v1:
time: 817 us; the launch traced here: 816 us
  waiting for transfers between devices  619 us (76%)
  starting transfers between devices  82.1 us (10%)
  other arithmetic  40.4 us (5%)
  local copies, waits for them, and re-layouts  38.2 us (5%)
  between operations  17.2 us (2%)
  blocking collectives  15.8 us (2%)
    psum x2, waiting for transfers between devices, shards(): gram = lax.psum(lax.psum(gram_local, 'tiles'), 'vec')  592 us
    ppermute x20, starting transfers between devices, shifted(): lax.ppermute(value, axis, [(source, source + steps) for source in range(f...  82 us
    ppermute x20, waiting for transfers between devices, shifted(): lax.ppermute(value, axis, [(source, source + steps) for source in range(f...  27.8 us
  transfers between devices with their start and end apart: 22, of which 15 were waited for; matrix products, arithmetic and copies ran while one was open for 1% of the time, Pallas kernels for 0%

profile of v1, /device:TPU:1, one launch (start us, length us, event | category | flops | bytes accessed | tf_op | source)
XLA Modules:
  0.0 816.0 jit_solution(3874081718535081895)
XLA Ops:
  7.2 1.5 fusion.34
  13.2 0.8 slice_multiply_fusion.2
  14.1 6.3 collective-permute-start
  20.4 1.3 collective-permute-start.1
  21.7 1.8 copy_multiply_fusion
  23.6 2.7 collective-permute-done.1
  26.4 5.1 collective-permute-start.2
  31.6 1.9 collective-permute-start.3
  33.5 3.2 collective-permute-start.4
  36.7 1.3 collective-permute-start.5
  38.6 5.3 collective-permute-done.5
  44.0 1.5 fusion.28
  45.6 2.0 copy.15
  48.3 8.0 collective-permute-start.7
  56.2 1.9 collective-permute-start.6
  58.4 1.0 collective-permute-done.6
  59.8 1.6 copy.18
  61.4 2.4 pad_maximum_fusion
  64.6 0.9 copy-done.1
  66.7 1.3 fusion.23
  68.0 6.0 collective-permute-start.8
  74.1 1.3 collective-permute-start.9
  76.0 5.3 collective-permute-done.9
  81.4 1.5 fusion.27
  82.9 2.0 copy.21
  84.9 5.5 collective-permute-start.10
  91.1 5.1 collective-permute-start.11
  96.9 1.6 copy.24
  98.4 2.4 pad_maximum_fusion.1
  101.6 0.9 copy-done.2
  103.3 1.3 fusion.20
  104.7 4.5 collective-permute-start.12
  109.2 1.3 collective-permute-start.13
  111.1 5.3 collective-permute-done.13
  116.5 1.5 fusion.26
  118.0 2.0 copy.27
  120.0 1.9 collective-permute-start.14
  122.6 8.8 %collective-permute-start.15 = (f32[64,4,10,1]{0,2,3,1:T(8,128)S(1)}, f32[64,4,10,1]{0,2,3,1:T(8,128)S(1)}, u32[]{:S(2)}, u32[]{:S(2)}) collective-permute-start(f32[64,4,10,1]{0,2,3,1:T(8,128)S(1)} %copy.28), channel_id=1, source_target_pairs={{2,0},{4,2},{6,4},{8,6},{10,8},{12,10},{14,12},{16,14},{18,16},{20... | collective-permute-start | bytes 30728 | tf_op jit(solution)/shard_map/ppermute | solution.py:13
  132.3 1.6 copy.30
  133.8 2.4 pad_maximum_fusion.2
  137.1 0.9 copy-done.3
  138.8 1.3 fusion.17
  140.1 6.4 collective-permute-start.16
  146.5 1.3 collective-permute-start.17
  148.4 5.3 collective-permute-done.17
  153.8 1.5 fusion.25
  155.3 2.0 copy.33
  157.3 1.9 collective-permute-start.18
  159.9 9.0 %collective-permute-start.19 = (f32[64,4,10,1]{0,2,3,1:T(8,128)S(1)}, f32[64,4,10,1]{0,2,3,1:T(8,128)S(1)}, u32[]{:S(2)}, u32[]{:S(2)}) collective-permute-start(f32[64,4,10,1]{0,2,3,1:T(8,128)S(1)} %copy.34), channel_id=1, source_target_pairs={{2,0},{4,2},{6,4},{8,6},{10,8},{12,10},{14,12},{16,14},{18,16},{20... | collective-permute-start | bytes 30728 | tf_op jit(solution)/shard_map/ppermute | solution.py:13
  169.6 1.6 copy.36
  171.1 2.4 pad_maximum_fusion.3
  174.3 0.9 copy-done
  176.0 1.3 fusion.14
  178.0 15.8 %all_to_all.15 = f32[64,4,8,128]{3,2,0,1:T(8,128)S(1)} all-to-all(f32[64,4,8,128]{3,2,0,1:T(8,128)S(1)} %copy.39), channel_id=1, replica_groups=mesh['tiles'=64,'vec'=2] {'vec'}, dimensions={1} | all-to-all | bytes 2097152 | tf_op jit(solution)/shard_map/all_to_all | solution.py:80
  193.8 1.1 copy.52
  194.9 1.4 reshape.96
  196.3 1.1 mul.184
  197.5 2.9 convolution_multiply_fusion
  200.4 564.2 %all-reduce.11.cloned.1.call-done = f32[128,128]{0,1:T(8,128)} async-done(((f32[128,128]{0,1:T(8,128)}), f32[128,128]{0,1:T(8,128)}) %all-reduce.11.cloned.1.call-update) | async-done | bytes 65552 | tf_op jit(solution)/shard_map/psum | solution.py:95
  764.6 1.6 copy.43
  766.2 27.4 %all-reduce.13.cloned.1.call-done = f32[128,128]{0,1:T(8,128)} async-done(((f32[128,128]{0,1:T(8,128)}), f32[128,128]{0,1:T(8,128)}) %all-reduce.13.cloned.1.call-update) | async-done | bytes 65552 | tf_op jit(solution)/shard_map/psum | solution.py:95
  793.6 0.9 copy.42
  794.5 0.9 fusion.24
  795.4 11.7 %cholesky.18 = f32[128,128]{1,0:T(8,128)S(1)} custom-call(f32[128,128]{1,0:T(8,128)S(1)} %fusion.24), custom_call_target="Cholesky" | custom-call | tf_op jit(solution)/shard_map/jit(cholesky)/cholesky | solution.py:96
  (83 shorter events, 20.1 us)
Async XLA Ops:
  7.2 757.5 %all-reduce.11.cloned.1.call-start = ((), (), s32[]{:S(2)}) async-start(), calls=%async_computation.1 | async-start | bytes 131072 | tf_op jit(solution)/shard_map/psum | solution.py:95
  14.1 9.5 %collective-permute-start = (f32[4,4,1,128]{3,2,1,0:T(1,128)S(1)}, f32[4,4,1,128]{3,2,1,0:T(1,128)S(1)}, u32[]{:S(2)}, u32[]{:S(2)}) collective-permute-start(f32[4,4,1,128]{3,2,1,0:T(1,128)S(1)} %get-tuple-element.29), channel_id=1, source_target_pairs={{0,16},{2,18},{4,20},{6,22},{8,24},{10,26},{12,28},{14,30},{16,32}... | collective-permute-start | bytes 24584 | tf_op jit(solution)/shard_map/ppermute | solution.py:13
  20.4 5.9 collective-permute-start.1
  26.4 11.6 %collective-permute-start.2 = (f32[4,4,10,1]{3,2,1,0:T(8,128)S(1)}, f32[4,4,10,1]{3,2,1,0:T(8,128)S(1)}, u32[]{:S(2)}, u32[]{:S(2)}) collective-permute-start(f32[4,4,10,1]{3,2,1,0:T(8,128)S(1)} %get-tuple-element.27), channel_id=1, source_target_pairs={{0,2},{2,4},{4,6},{6,8},{8,10},{10,12},{12,14},{14,16},{16,18},{18... | collective-permute-start | bytes 1928 | tf_op jit(solution)/shard_map/ppermute | solution.py:13
  31.6 6.5 collective-permute-start.3
  33.5 5.1 collective-permute-start.4
  36.7 7.2 collective-permute-start.5
  48.3 11.5 %collective-permute-start.7 = (f32[64,4,10,1]{0,2,3,1:T(8,128)S(1)}, f32[64,4,10,1]{0,2,3,1:T(8,128)S(1)}, u32[]{:S(2)}, u32[]{:S(2)}) collective-permute-start(f32[64,4,10,1]{0,2,3,1:T(8,128)S(1)} %copy.16), channel_id=1, source_target_pairs={{2,0},{4,2},{6,4},{8,6},{10,8},{12,10},{14,12},{16,14},{18,16},{20... | collective-permute-start | bytes 30728 | tf_op jit(solution)/shard_map/ppermute | solution.py:13
  56.2 3.1 collective-permute-start.6
  58.2 42.7 %copy-start.5 = (f32[3,10,130]{2,1,0:T(8,128)}, f32[3,10,130]{2,1,0:T(8,128)S(1)}, u32[]{:S(2)}) copy-start(f32[3,10,130]{2,1,0:T(8,128)S(1)} %slice_bitcast_fusion.3) | copy-start | bytes 46804
  64.1 1.3 copy-start.1
  65.5 1.2 copy-start.4
  68.0 8.0 collective-permute-start.8
  74.1 7.2 collective-permute-start.9
  84.9 11.3 %collective-permute-start.10 = (f32[64,4,10,1]{0,2,3,1:T(8,128)S(1)}, f32[64,4,10,1]{0,2,3,1:T(8,128)S(1)}, u32[]{:S(2)}, u32[]{:S(2)}) collective-permute-start(f32[64,4,10,1]{0,2,3,1:T(8,128)S(1)} %copy.21), channel_id=1, source_target_pairs={{0,2},{2,4},{4,6},{6,8},{8,10},{10,12},{12,14},{14,16},{16,18},{18... | collective-permute-start | bytes 30728 | tf_op jit(solution)/shard_map/ppermute | solution.py:13
  91.1 5.8 collective-permute-start.11
  101.2 1.3 copy-start.2
  104.7 6.4 collective-permute-start.12
  109.2 7.2 collective-permute-start.13
  120.0 11.4 %collective-permute-start.14 = (f32[64,4,10,1]{0,2,3,1:T(8,128)S(1)}, f32[64,4,10,1]{0,2,3,1:T(8,128)S(1)}, u32[]{:S(2)}, u32[]{:S(2)}) collective-permute-start(f32[64,4,10,1]{0,2,3,1:T(8,128)S(1)} %copy.27), channel_id=1, source_target_pairs={{0,2},{2,4},{4,6},{6,8},{8,10},{10,12},{12,14},{14,16},{16,18},{18... | collective-permute-start | bytes 30728 | tf_op jit(solution)/shard_map/ppermute | solution.py:13
  122.6 9.6 %collective-permute-start.15 = (f32[64,4,10,1]{0,2,3,1:T(8,128)S(1)}, f32[64,4,10,1]{0,2,3,1:T(8,128)S(1)}, u32[]{:S(2)}, u32[]{:S(2)}) collective-permute-start(f32[64,4,10,1]{0,2,3,1:T(8,128)S(1)} %copy.28), channel_id=1, source_target_pairs={{2,0},{4,2},{6,4},{8,6},{10,8},{12,10},{14,12},{16,14},{18,16},{20... | collective-permute-start | bytes 30728 | tf_op jit(solution)/shard_map/ppermute | solution.py:13
  133.8 2.4 copy-start.6
  136.6 1.3 copy-start.3
  140.1 8.3 %collective-permute-start.16 = (f32[64,4,1,128]{3,0,2,1:T(8,128)S(1)}, f32[64,4,1,128]{3,0,2,1:T(8,128)S(1)}, u32[]{:S(2)}, u32[]{:S(2)}) collective-permute-start(f32[64,4,1,128]{3,0,2,1:T(8,128)S(1)} %get-tuple-element.16), channel_id=1, source_target_pairs={{0,16},{2,18},{4,20},{6,22},{8,24},{10,26},{12,28},{14,30},{16,32}... | collective-permute-start | bytes 393224 | tf_op jit(solution)/shard_map/ppermute | solution.py:13
  146.5 7.2 collective-permute-start.17
  157.3 11.7 %collective-permute-start.18 = (f32[64,4,10,1]{0,2,3,1:T(8,128)S(1)}, f32[64,4,10,1]{0,2,3,1:T(8,128)S(1)}, u32[]{:S(2)}, u32[]{:S(2)}) collective-permute-start(f32[64,4,10,1]{0,2,3,1:T(8,128)S(1)} %copy.33), channel_id=1, source_target_pairs={{0,2},{2,4},{4,6},{6,8},{8,10},{10,12},{12,14},{14,16},{16,18},{18... | collective-permute-start | bytes 30728 | tf_op jit(solution)/shard_map/ppermute | solution.py:13
  159.9 9.6 %collective-permute-start.19 = (f32[64,4,10,1]{0,2,3,1:T(8,128)S(1)}, f32[64,4,10,1]{0,2,3,1:T(8,128)S(1)}, u32[]{:S(2)}, u32[]{:S(2)}) collective-permute-start(f32[64,4,10,1]{0,2,3,1:T(8,128)S(1)} %copy.34), channel_id=1, source_target_pairs={{2,0},{4,2},{6,4},{8,6},{10,8},{12,10},{14,12},{16,14},{18,16},{20... | collective-permute-start | bytes 30728 | tf_op jit(solution)/shard_map/ppermute | solution.py:13
  171.1 2.4 copy-start.7
  173.9 1.3 copy-start
  178.0 16.9 %copy-start.8 = (f32[8,128]{1,0:T(8,128)S(1)}, f32[8,128]{1,0:T(8,128)}, u32[]{:S(2)}) copy-start(f32[8,128]{1,0:T(8,128)} %param.8) | copy-start | bytes 12292
  200.3 593.3 %all-reduce.13.cloned.1.call-start = ((), (), s32[]{:S(2)}) async-start(), calls=%async_computation.2 | async-start | bytes 131072 | tf_op jit(solution)/shard_map/psum | solution.py:95
Sparse Core Ops, SparseCore 0:
  200.5 564.1 all-reduce.10
  767.0 26.5 all-reduce.12
